TPU v7x, 32 devices: a whole 2x2x4 slice. The times are simulated.
32 devices in a mesh: gx: 8 (over y, x, core), row: 4 (over z).
Axes of the slice: x: 2, y: 2, z: 4, core: 2. Of those that a mesh axis runs over, the one named last changes fastest.
Arguments:
- amplitudes: float32 [128, 4096], P('gx', 'row'), may hold values from -6 to 6
- integrals: float32 [4096, 16384], P('row', 'gx'), may hold values from -0.1875 to 0.1875
- cd_irrep: int32 [32], P('row'), may hold values from 0 to 7
- ab_irrep: int32 [128], P('gx'), may hold values from 0 to 7
- allowed: int32 [8, 8], replicated, may hold values 0 or 1
- pair_occ: int32 [128, 2], P(('gx', 'row')), may hold values from 0 to 99
- occ_energy: float32 [100], replicated, may hold values from -1 to -0.25
- ab_energy: float32 [16384], replicated, may hold values from 1 to 4
Outputs:
- residual: float32 [128, 16384], P(('gx', 'row'))
- update: float32 [128, 16384], P(('gx', 'row'))
All inputs are finite; a program needn't handle non-finite values.
Results may differ from a plain program's by a relative error of at most 0.000071.
Values sent between devices are 32-bit elements; how exact they have to be, the bound alone decides.
A program may use at most 128 MiB of HBM per device.

v0:
```python
import functools

import jax
import jax.numpy as jnp
from jax import lax
from jax.experimental import pallas as pl
from jax.experimental.pallas import tpu as pltpu
from jax.sharding import PartitionSpec as P

BLK = 128
MESH = pl.DeviceIdType.MESH
VMEM_BUDGET = 48 * 2**20
VMEM_GRANT = 67043328


def plain_body(amplitudes, integrals, cd_irrep, ab_irrep, allowed, pair_occ, occ_energy, ab_energy):
    irrep_labels = jnp.arange(allowed.shape[0], dtype=jnp.int32)
    cd_onehot = (cd_irrep[:, None] == irrep_labels[None, :]).astype(jnp.float32)
    ab_onehot = (ab_irrep[:, None] == irrep_labels[None, :]).astype(jnp.float32)
    irrep_table = allowed.astype(jnp.float32)
    block_mask = jnp.dot(
        jnp.dot(cd_onehot, irrep_table, precision=lax.Precision.HIGHEST),
        ab_onehot.T,
        precision=lax.Precision.HIGHEST,
    )
    cd_rows, ab_cols = integrals.shape
    effective = (
        integrals.reshape(cd_rows // BLK, BLK, ab_cols // BLK, BLK) * block_mask[:, None, :, None]
    ).reshape(cd_rows, ab_cols)
    partial_value = jnp.dot(
        lax.all_gather(amplitudes, "gx", axis=0, tiled=True),
        effective,
        precision=lax.Precision.HIGHEST,
        preferred_element_type=jnp.float32,
    )
    arrived = lax.all_to_all(partial_value, "gx", split_axis=0, concat_axis=1, tiled=True)
    residual = lax.psum_scatter(arrived, "row", scatter_dimension=0, tiled=True)
    occ_labels = jnp.arange(occ_energy.shape[0], dtype=jnp.int32)
    pair_onehot = (pair_occ[:, :, None] == occ_labels[None, None, :]).astype(jnp.float32)
    pair_energy = jnp.sum(pair_onehot * occ_energy[None, None, :], axis=(1, 2))
    update = residual / (ab_energy[None, :] - pair_energy[:, None])
    return (residual, update)


def kernel(
    N, Z, T, W, L,
    amp, integ, cd_in, ab_in, allowed_in,
    res_out,
    cd, ab, allowed, small_sem, amp_sem,
    raw, wh, wl, gathered, ordered, a2, own, arrive, fin,
    isem, ag_send, ag_recv, relay_send, zsend, zrecv, xsend, xrecv, own_sem,
):
    g = lax.axis_index("gx")
    z = lax.axis_index("row")
    rows, K = amp.shape
    half, Zh = rows // 2, Z // 2
    HP = half * N
    pk = rows // Z
    far = jnp.where(z < Zh, 1, 0)
    partner = g + 1 - 2 * lax.rem(g, 2)
    parity = lax.rem(g, 2)

    def load(t):
        cols = pl.ds(pl.multiple_of(t * W, W), W)
        return pltpu.make_async_copy(integ.at[:, cols], raw.at[t], isem.at[t])

    def own_amp(h):
        return pltpu.make_async_copy(
            amp.at[pl.ds(pl.multiple_of(h * half, half), half), :], gathered.at[g, h], amp_sem.at[h])

    own_amp(far).start()
    own_amp(1 - far).start()
    small = [
        pltpu.make_async_copy(src, dst, small_sem.at[i])
        for i, (src, dst) in enumerate((
            (cd_in, cd), (ab_in, ab), (allowed_in, allowed)))
    ]
    for c in small:
        c.start()
    barrier = pltpu.get_barrier_semaphore()
    for j in range(1, N):
        pl.semaphore_signal(barrier, inc=1, device_id={"gx": lax.rem(g + j, N)}, device_id_type=MESH)

    @pl.when(z > 0)
    def _():
        pl.semaphore_signal(barrier, inc=1, device_id={"row": z - 1}, device_id_type=MESH)

    @pl.when(z < Z - 1)
    def _():
        pl.semaphore_signal(barrier, inc=1, device_id={"row": z + 1}, device_id_type=MESH)

    nearby = jnp.where(z > 0, 1, 0) + jnp.where(z < Z - 1, 1, 0)
    pl.semaphore_wait(barrier, N - 1 + nearby)

    def send_own(peer, h):
        return pltpu.make_async_remote_copy(
            src_ref=gathered.at[g, h], dst_ref=gathered.at[g, h], send_sem=ag_send.at[h, peer],
            recv_sem=ag_recv.at[h, g], device_id={"gx": peer}, device_id_type=MESH)

    def relay(s, h):
        return pltpu.make_async_remote_copy(
            src_ref=gathered.at[s, h], dst_ref=gathered.at[s, h], send_sem=relay_send.at[h, s],
            recv_sem=ag_recv.at[h, s], device_id={"gx": partner}, device_id_type=MESH)

    like = [lax.rem(g + 2 * j, N) for j in range(N // 2 - 1, 0, -1)]
    for h in (far, 1 - far):
        own_amp(h).wait()
        for peer in like:
            send_own(peer, h).start()
        send_own(partner, h).start()
    for t in range(T):
        load(t).start()
    for c in small:
        c.wait()

    KB = K // BLK
    WB = W // BLK

    def split(t, carry):
        load(t).wait()
        for b in range(KB):
            for j in range(WB):
                m = allowed[cd[b], ab[t * WB + j]].astype(jnp.float32)
                x = raw[t, b * BLK:(b + 1) * BLK, j * BLK:(j + 1) * BLK] * m
                hi = x.astype(jnp.bfloat16)
                wh[t, b * BLK:(b + 1) * BLK, j * BLK:(j + 1) * BLK] = hi
                wl[t, b * BLK:(b + 1) * BLK, j * BLK:(j + 1) * BLK] = (x - hi.astype(jnp.float32)).astype(jnp.bfloat16)
        return carry

    lax.fori_loop(0, T, split, 0)

    def forward(h):
        for s in like[::-1]:
            relay(s, h).wait_recv()
            relay(s, h).start()

    def prepare(h):
        relay(partner, h).wait_recv()
        for j in range(1, N // 2):
            relay(lax.rem(partner + 2 * j, N), h).wait_recv()
        for r in range(Zh):
            for s in range(N):
                at = (r * N + s) * pk
                ordered[at:at + pk, :] = gathered[s, h, r * pk:(r + 1) * pk, :]
        x = ordered[...]
        hi = x.astype(jnp.bfloat16)
        a2[0:HP, :] = hi
        a2[HP:2 * HP, :] = (x - hi.astype(jnp.float32)).astype(jnp.bfloat16)

    forward(far)
    prepare(far)

    RP = N * pk

    def send_z(d, t, up):
        to = z + 1 if up else z - 1
        side = 0 if up else 1
        return pltpu.make_async_remote_copy(
            src_ref=own.at[d, t], dst_ref=arrive.at[side, d, t], send_sem=zsend.at[d, t],
            recv_sem=zrecv.at[side, d, t], device_id={"row": to}, device_id_type=MESH)

    def compute(t, h):
        both = jnp.dot(a2[...], wh[t], preferred_element_type=jnp.float32)
        tail = jnp.dot(a2[0:HP, :], wl[t], preferred_element_type=jnp.float32)
        total = both[0:HP] + both[HP:2 * HP] + tail
        for r in range(Zh):
            own[h * Zh + r, t] = total[r * RP:(r + 1) * RP, :]

    def take(d, t, up):
        side = 0 if up else 1
        send_z(d, t, up).wait_recv()
        own[d, t] = own[d, t] + arrive[side, d, t]

    def place(s, t):
        return pl.ds(pl.multiple_of((s * T + t) * W, W), W)

    def keep(t):
        return pltpu.make_async_copy(fin.at[g, t], res_out.at[:, place(g, t)], own_sem.at[t])

    def to_peer(peer, t):
        return pltpu.make_async_remote_copy(
            src_ref=fin.at[peer, t], dst_ref=res_out.at[:, place(g, t)], send_sem=xsend.at[peer], recv_sem=xrecv.at[g],
            device_id={"gx": peer}, device_id_type=MESH)

    def close(t):
        @pl.when(z > 0)
        def _():
            take(z, t, True)

        @pl.when(z < Z - 1)
        def _():
            take(z, t, False)

        total = own[z, t]
        for s in range(N):
            fin[s, t] = total[s * pk:(s + 1) * pk, :]
        for j in range(1, N):
            to_peer(lax.rem(g + j, N), t).start()
        keep(t).start()

    last = Z - 1 - z
    lag_up, lag_down = z * L, last * L
    first_close = jnp.maximum(last * T + lag_up, z * T + lag_down)

    def step(s, carry):
        @pl.when(s == T // 4)
        def _():
            forward(1 - far)

        @pl.when(s == T)
        def _():
            prepare(1 - far)

        @pl.when(s < 2 * T)
        def _():
            compute(lax.rem(s, T), jnp.where(s < T, far, 1 - far))

        qu = s - lag_up

        @pl.when(jnp.logical_and(qu >= 0, qu < last * T))
        def _():
            d, t = Z - 1 - qu // T, lax.rem(qu, T)

            @pl.when(z > 0)
            def _():
                take(d, t, True)

            send_z(d, t, True).start()

        qd = s - lag_down

        @pl.when(jnp.logical_and(qd >= 0, qd < z * T))
        def _():
            d, t = qd // T, lax.rem(qd, T)

            @pl.when(z < Z - 1)
            def _():
                take(d, t, False)

            send_z(d, t, False).start()

        tc = s - first_close

        @pl.when(jnp.logical_and(tc >= 0, tc < T))
        def _():
            close(tc)

        return carry

    lax.fori_loop(0, Z * T + (Z - 1) * L, step, 0)

    def whole(s):
        band = res_out.at[:, pl.ds(pl.multiple_of(s * T * W, W), T * W)]
        return pltpu.make_async_remote_copy(
            src_ref=band, dst_ref=band, send_sem=xsend.at[s], recv_sem=xrecv.at[s],
            device_id={"gx": s}, device_id_type=MESH)

    for peer in like:
        for h in range(2):
            send_own(peer, h).wait_send()
            relay(peer, h).wait_send()
    for h in range(2):
        send_own(partner, h).wait_send()

    def collect(j, carry):
        whole(lax.rem(g + j, N)).wait_recv()
        return carry

    lax.fori_loop(1, N, collect, 0)

    def drain_own(t, carry):
        keep(t).wait()
        return carry

    lax.fori_loop(0, T, drain_own, 0)

    def drain(j, carry):
        whole(lax.rem(g + j, N)).wait_send()
        return carry

    lax.fori_loop(1, N, drain, 0)
    for d in range(Z):
        @pl.when(z != d)
        def _():
            def drain_z(t, carry):
                send_z(d, t, True).wait_send()
                return carry
            lax.fori_loop(0, T, drain_z, 0)


def divide(res, pair_occ, occ, energy, res_out, upd_out):
    pk, A = res.shape
    which = lax.broadcasted_iota(jnp.int32, (pk, 1), 0)
    pe = jnp.zeros((pk, 1), jnp.float32)
    for k in range(pk):
        pe = jnp.where(which == k, occ[pair_occ[0, k]] + occ[pair_occ[1, k]], pe)
    v = res[...]
    res_out[...] = v
    upd_out[...] = v / (energy[...] - pe)


def fused_body(N, Z, W, L, amplitudes, integrals, cd_irrep, ab_irrep, allowed, pair_occ, occ_energy, ab_energy):
    rows, K = amplitudes.shape
    AB = integrals.shape[1]
    A = ab_energy.shape[0]
    T = AB // W
    pk = rows // Z
    RP = N * pk
    HP = rows * N // 2
    vmem, smem = pltpu.VMEM, pltpu.SMEM
    f32, bf16, i32 = jnp.float32, jnp.bfloat16, jnp.int32
    dma = pltpu.SemaphoreType.DMA
    out = jax.ShapeDtypeStruct((pk, A), f32)
    residual = pl.pallas_call(
        functools.partial(kernel, N, Z, T, W, L),
        out_shape=out,
        in_specs=[pl.BlockSpec(memory_space=pltpu.HBM)] * 5,
        out_specs=pl.BlockSpec(memory_space=pltpu.HBM),
        scratch_shapes=[
            smem(cd_irrep.shape, i32), smem(ab_irrep.shape, i32), smem(allowed.shape, i32), dma((3,)), dma((2,)),
            vmem((T, K, W), f32), vmem((T, K, W), bf16), vmem((T, K, W), bf16),
            vmem((N, 2, rows // 2, K), f32), vmem((HP, K), f32), vmem((2 * HP, K), bf16),
            vmem((Z, T, RP, W), f32), vmem((2, Z, T, RP, W), f32), vmem((N, T, pk, W), f32),
            dma((T,)), dma((2, N)), dma((2, N)), dma((2, N)), dma((Z, T)), dma((2, Z, T)), dma((N,)), dma((N,)),
            dma((T,)),
        ],
        compiler_params=pltpu.CompilerParams(
            collective_id=0, has_side_effects=True, vmem_limit_bytes=VMEM_GRANT),
    )(amplitudes, integrals, cd_irrep, ab_irrep, allowed)
    return pl.pallas_call(
        divide,
        out_shape=(out, out),
        in_specs=[pl.BlockSpec(memory_space=s) for s in (vmem, smem, smem, vmem)],
        out_specs=[pl.BlockSpec(memory_space=vmem)] * 2,
        compiler_params=pltpu.CompilerParams(vmem_limit_bytes=VMEM_GRANT),
    )(residual, pair_occ.T, occ_energy, ab_energy.reshape(1, A))


def solution(mesh):
    N, Z = mesh.shape["gx"], mesh.shape["row"]

    def body(amplitudes, integrals, *rest):
        rows, K = amplitudes.shape
        AB = integrals.shape[1]
        W = 2 * BLK
        L = max(3, pl.cdiv(2 * (AB // W), Z))
        pk = rows // Z
        need = 8 * K * AB + 16 * rows * N * K + 12 * rows * N * AB + 24 * pk * AB * N
        if need > VMEM_BUDGET * 3 // 4 or AB % W or N % 2 or Z % 2 or rows % Z or rows % 16:
            return plain_body(amplitudes, integrals, *rest)
        return fused_body(N, Z, W, L, amplitudes, integrals, *rest)

    return jax.shard_map(
        body,
        mesh=mesh,
        in_specs=(
            P("gx", "row"),
            P("row", "gx"),
            P("row"),
            P("gx"),
            P(),
            P(("gx", "row"), None),
            P(),
            P(),
        ),
        out_specs=(P(("gx", "row"), None), P(("gx", "row"), None)),
        check_vma=False,
    )
```

profile of v0, /device:TPU:17, one launch (start us, length us, event | category | flops | bytes accessed | tf_op | source)
XLA Modules:
  0.0 34.2 jit_solution(4076760579978533054)
XLA Ops:
  0.6 31.8 %shard_map.95.res = f32[4,16384]{1,0:T(4,128)} custom-call(f32[16,1024]{1,0:T(8,128)} %amp.1, f32[1024,2048]{1,0:T(8,128)} %integ.1, s32[8]{0:T(128)} %cd_in.1, s32[16]{0:T(128)} %ab_in.1, s32[8,8]{1,0:T(8,128)} %allowed_in.1), custom_call_target="tpu_custom_call" | custom-call | tf_op jit(solution)/shard_map/pallas_call | solution.py:314
  32.5 1.8 %shard_map.96 = (f32[4,16384]{1,0:T(4,128)}, f32[4,16384]{1,0:T(4,128)}) custom-call(f32[4,16384]{1,0:T(4,128)} %shard_map.95.res, s32[2,4]{1,0:T(2,128)} %bitcast.3, f32[100]{0:T(128)} %occ.1, f32[1,16384]{1,0:T(1,128)} %bitcast.2), custom_call_target="tpu_custom_call" | custom-call | tf_op jit(solution)/shard_map/pallas_call | solution.py:330
where the time goes:
time: 34.4 us; the launch traced here: 34.2 us
  Pallas kernels  33.6 us (98%)
  between operations  0.64 us (2%)
    pallas_call x1, Pallas kernels, fused_body(): pl.pallas_call(functools.partial(kernel, N, Z, T, W, L), out_shape=out, i...  31.8 us
    pallas_call x1, Pallas kernels, fused_body(): pl.pallas_call(divide, out_shape=(out, out), in_specs=[pl.BlockSpec(memor...  1.78 us

commit v1 on v0

v1 whole, which is shorter than its diff:
```python
import functools

import jax
import jax.numpy as jnp
from jax import lax
from jax.experimental import pallas as pl
from jax.experimental.pallas import tpu as pltpu
from jax.sharding import PartitionSpec as P

BLK = 128
MESH = pl.DeviceIdType.MESH
VMEM_BUDGET = 48 * 2**20
VMEM_GRANT = 67043328
LAGS = (11, 5)


def plain_body(amplitudes, integrals, cd_irrep, ab_irrep, allowed, pair_occ, occ_energy, ab_energy):
    irrep_labels = jnp.arange(allowed.shape[0], dtype=jnp.int32)
    cd_onehot = (cd_irrep[:, None] == irrep_labels[None, :]).astype(jnp.float32)
    ab_onehot = (ab_irrep[:, None] == irrep_labels[None, :]).astype(jnp.float32)
    irrep_table = allowed.astype(jnp.float32)
    block_mask = jnp.dot(
        jnp.dot(cd_onehot, irrep_table, precision=lax.Precision.HIGHEST),
        ab_onehot.T,
        precision=lax.Precision.HIGHEST,
    )
    cd_rows, ab_cols = integrals.shape
    effective = (
        integrals.reshape(cd_rows // BLK, BLK, ab_cols // BLK, BLK) * block_mask[:, None, :, None]
    ).reshape(cd_rows, ab_cols)
    partial_value = jnp.dot(
        lax.all_gather(amplitudes, "gx", axis=0, tiled=True),
        effective,
        precision=lax.Precision.HIGHEST,
        preferred_element_type=jnp.float32,
    )
    arrived = lax.all_to_all(partial_value, "gx", split_axis=0, concat_axis=1, tiled=True)
    residual = lax.psum_scatter(arrived, "row", scatter_dimension=0, tiled=True)
    occ_labels = jnp.arange(occ_energy.shape[0], dtype=jnp.int32)
    pair_onehot = (pair_occ[:, :, None] == occ_labels[None, None, :]).astype(jnp.float32)
    pair_energy = jnp.sum(pair_onehot * occ_energy[None, None, :], axis=(1, 2))
    update = residual / (ab_energy[None, :] - pair_energy[:, None])
    return (residual, update)


def kernel(
    N, Z, T, W,
    amp, integ, cd_in, ab_in, allowed_in,
    res_out,
    cd, ab, allowed, small_sem, amp_sem,
    raw, wh, wl, gathered, ordered, near_lhs, side_lhs, far_lhs,
    own, from_edge, from_mid, from_in, fin, efin, base, ebuf, last, res,
    isem, ag_send, ag_recv, stream_send, edge_recv, mid_recv, back_send,
    fin_send, base_recv, efin_send, last_send, last_recv, out_sem,
):
    g = lax.axis_index("gx")
    z = lax.axis_index("row")
    rows, K = amp.shape
    half = rows // 2
    pk = rows // Z
    C = N // 2
    U = T // 2
    lower = z < Z // 2
    edge = jnp.logical_or(z == 0, z == Z - 1)
    inner = jnp.logical_not(edge)
    inward = jnp.where(lower, z + 1, z - 1)
    outward = jnp.where(lower, z - 1, z + 1)
    chip, core = g // 2, lax.rem(g, 2)

    def peer(c, i):
        there = lax.rem(chip // 2 + c // 2, 2) * 2 + lax.rem(lax.rem(chip, 2) + lax.rem(c, 2), 2)
        return there * 2 + (core if i == 0 else 1 - core)

    partner = peer(0, 1)

    def load(t):
        cols = pl.ds(pl.multiple_of(t * W, W), W)
        return pltpu.make_async_copy(integ.at[:, cols], raw.at[t], isem.at[t])

    def own_amp(h):
        return pltpu.make_async_copy(amp.at[pl.ds(h * half, half), :], gathered.at[g, h], amp_sem)

    own_amp(0).start()
    own_amp(1).start()
    small = [
        pltpu.make_async_copy(src, dst, small_sem.at[i])
        for i, (src, dst) in enumerate((
            (cd_in, cd), (ab_in, ab), (allowed_in, allowed)))
    ]
    for c in small:
        c.start()
    load(0).start()
    barrier = pltpu.get_barrier_semaphore()
    close = [partner, peer(1, 0), peer(2, 0)]
    for to in close:
        pl.semaphore_signal(barrier, inc=1, device_id={"gx": to}, device_id_type=MESH)
    pl.semaphore_signal(barrier, inc=1, device_id={"row": inward}, device_id_type=MESH)

    @pl.when(inner)
    def _():
        pl.semaphore_signal(barrier, inc=1, device_id={"row": outward}, device_id_type=MESH)

    def send_own(to, h):
        return pltpu.make_async_remote_copy(
            src_ref=gathered.at[g, h], dst_ref=gathered.at[g, h], send_sem=ag_send,
            recv_sem=ag_recv.at[h, g], device_id={"gx": to}, device_id_type=MESH)

    def relay(s, h):
        return pltpu.make_async_remote_copy(
            src_ref=gathered.at[s, h], dst_ref=gathered.at[s, h], send_sem=ag_send,
            recv_sem=ag_recv.at[h, s], device_id={"gx": partner}, device_id_type=MESH)

    def cross(s, h, to):
        return pltpu.make_async_remote_copy(
            src_ref=gathered.at[s, h], dst_ref=gathered.at[s, h], send_sem=ag_send,
            recv_sem=ag_recv.at[h, s], device_id={"gx": to}, device_id_type=MESH)

    across, along, opposite = peer(1, 0), peer(2, 0), peer(3, 0)

    def spread():
        for h in range(2):
            send_own(partner, h).start()
        for h in range(2):
            send_own(across, h).start()
            send_own(along, h).start()

    def forward_side():
        for h in range(2):
            relay(across, h).wait_recv()
            if h == 0:
                cross(across, h, along).start()
            relay(across, h).start()
            relay(along, h).wait_recv()
            if h == 1:
                cross(along, h, across).start()
            relay(along, h).start()

    def forward_diag():
        for h in range(2):
            relay(opposite, h).wait_recv()
            relay(opposite, h).start()

    def arrived(cs):
        for c in cs:
            for h in range(2):
                relay(peer(c, 1), h).wait_recv()

    def prepare(cs, lhs):
        n = len(cs)
        M = n * 2 * rows
        for k in range(Z):
            for j, c in enumerate(cs):
                for i in range(2):
                    at = ((k * n + j) * 2 + i) * pk
                    s = peer(c, i)
                    up, down = (Z - 1 - k) * pk, k * pk
                    x = jnp.where(
                        lower,
                        gathered[s, up // half, up % half:up % half + pk, :],
                        gathered[s, down // half, down % half:down % half + pk, :])
                    ordered[at:at + pk, :] = x
        x = ordered[0:M, :]
        hi = x.astype(jnp.bfloat16)
        lhs[0:M, :] = hi
        lhs[M:2 * M, :] = (x - hi.astype(jnp.float32)).astype(jnp.bfloat16)

    KB = K // BLK
    WB = W // BLK

    def split(t):
        for b in range(KB):
            for j in range(WB):
                m = allowed[cd[b], ab[t * WB + j]].astype(jnp.float32)
                x = raw[t, b * BLK:(b + 1) * BLK, j * BLK:(j + 1) * BLK] * m
                hi = x.astype(jnp.bfloat16)
                wh[t, b * BLK:(b + 1) * BLK, j * BLK:(j + 1) * BLK] = hi
                wl[t, b * BLK:(b + 1) * BLK, j * BLK:(j + 1) * BLK] = (x - hi.astype(jnp.float32)).astype(jnp.bfloat16)

    def send_piece(c, i, t):
        return pltpu.make_async_remote_copy(
            src_ref=efin.at[c * 2 + i, t], dst_ref=ebuf.at[g, t], send_sem=efin_send, recv_sem=last_recv.at[g],
            device_id={"gx": peer(c, i)}, device_id_type=MESH)

    def send_tile(k, c, t):
        return pltpu.make_async_remote_copy(
            src_ref=own.at[k, c, t], dst_ref=from_edge.at[k, c, t], send_sem=stream_send,
            recv_sem=edge_recv.at[k, c, t // 2], device_id={"row": inward}, device_id_type=MESH)

    def send_last(s):
        return pltpu.make_async_remote_copy(
            src_ref=ebuf.at[s], dst_ref=last.at[s], send_sem=last_send, recv_sem=last_recv.at[s],
            device_id={"row": inward}, device_id_type=MESH)

    def compute(cs, lhs, t, ready=()):
        n = len(cs)
        M = n * 2 * rows
        R = 2 * pk
        both = jnp.dot(lhs[...], wh[t], preferred_element_type=jnp.float32)
        tail = jnp.dot(lhs[0:M, :], wl[t], preferred_element_type=jnp.float32)
        total = both[0:M] + both[M:2 * M] + tail
        for k in range(Z):
            for j, c in enumerate(cs):
                own[k, c, t] = total[(k * n + j) * R:(k * n + j + 1) * R, :]

        for k, c in ready:
            send_tile(k, c, t).start()
        if ready:
            for j, c in enumerate(cs):
                for i in range(2):
                    at = ((2 * n + j) * 2 + i) * pk
                    if c == 0 and i == 0:
                        ebuf[g, t] = total[at:at + pk, :]
                    else:
                        efin[c * 2 + i, t] = total[at:at + pk, :]
                        send_piece(c, i, t).start()

    def unit(i):
        seg, u, b = i // (2 * U), lax.rem(i, 2 * U) // 2, lax.rem(i, 2)
        k = jnp.where(seg == 0, b, jnp.where(seg == 1, 0, jnp.where(seg == 2, b, 1)))
        c = jnp.where(seg == 0, 0, jnp.where(seg == 1, 1 + b, jnp.where(seg == 2, 3 - 2 * b, 2 + b)))
        return k, c, u

    def pair(u):
        return pl.ds(u * 2, 2)

    def edge_unit(k, c, u):
        return pltpu.make_async_remote_copy(
            src_ref=own.at[k, c, pair(u)], dst_ref=from_edge.at[k, c, pair(u)], send_sem=stream_send,
            recv_sem=edge_recv.at[k, c, u], device_id={"row": inward}, device_id_type=MESH)

    def mid_unit(k, c, u):
        return pltpu.make_async_remote_copy(
            src_ref=own.at[k, c, pair(u)], dst_ref=from_mid.at[k, c, pair(u)], send_sem=stream_send,
            recv_sem=mid_recv.at[k, c, u], device_id={"row": inward}, device_id_type=MESH)

    def back_unit(c, u):
        return pltpu.make_async_remote_copy(
            src_ref=own.at[Z - 1, c, pair(u)], dst_ref=from_in.at[c, pair(u)], send_sem=back_send,
            recv_sem=mid_recv.at[0, c, u], device_id={"row": outward}, device_id_type=MESH)

    def base_unit(c, i, u):
        return pltpu.make_async_remote_copy(
            src_ref=fin.at[c * 2 + i, pair(u)], dst_ref=base.at[g, pair(u)], send_sem=fin_send,
            recv_sem=base_recv.at[g], device_id={"gx": peer(c, i)}, device_id_type=MESH)

    def scatter(c, u, total):
        @pl.when(c == 0)
        def _():
            base[g, pair(u)] = total[:, 0:pk, :]

        @pl.when(c > 0)
        def _():
            fin[c * 2, pair(u)] = total[:, 0:pk, :]
            base_unit(c, 0, u).start()

        fin[c * 2 + 1, pair(u)] = total[:, pk:2 * pk, :]
        base_unit(c, 1, u).start()

    def take_edge(i):
        k, c, u = unit(i)
        edge_unit(k, c, u).wait_recv()
        own[k, c, pair(u)] = own[k, c, pair(u)] + from_edge[k, c, pair(u)]
        mid_unit(k, c, u).start()

    def take_mid(i):
        k, c, u = unit(i)
        mid_unit(k, c, u).wait_recv()

        @pl.when(k == 0)
        def _():
            own[Z - 1, c, pair(u)] = own[Z - 1, c, pair(u)] + from_mid[0, c, pair(u)]
            back_unit(c, u).start()

        @pl.when(k == 1)
        def _():
            scatter(c, u, own[Z - 2, c, pair(u)] + from_mid[1, c, pair(u)])

    def take_back(i):
        j = i - U
        c = jnp.where(i < U, 0, jnp.where(i < 3 * U, 1 + lax.rem(j + 2 * U, 2), 3))
        u = jnp.where(i < U, i, jnp.where(i < 3 * U, j // 2, i - 3 * U))
        back_unit(c, u).wait_recv()
        scatter(c, u, own[Z - 1, c, pair(u)] + from_in[c, pair(u)])

    def whole_ebuf(s):
        return pltpu.make_async_remote_copy(
            src_ref=ebuf.at[s], dst_ref=ebuf.at[s], send_sem=last_send, recv_sem=last_recv.at[s],
            device_id={"gx": s}, device_id_type=MESH)

    def whole_base(s):
        return pltpu.make_async_remote_copy(
            src_ref=base.at[s], dst_ref=base.at[s], send_sem=last_send, recv_sem=base_recv.at[s],
            device_id={"gx": s}, device_id_type=MESH)

    near, side, diag = (0,), (1, 2), (3,)
    n_units = 2 * C * U

    def repeat(lo, hi, body):
        def once(t, carry):
            body(t)
            return carry
        lax.fori_loop(lo, hi, once, 0)

    def ready_tile(t):
        load(t).wait()
        split(t)

    pltpu.make_async_copy(gathered.at[g], gathered.at[g], amp_sem).wait()
    for c in small:
        c.wait()
    repeat(1, T, lambda t: load(t).start())
    pl.semaphore_wait(barrier, len(close) + jnp.where(edge, 1, 2))
    spread()
    repeat(0, T // 2, ready_tile)
    for h in range(2):
        relay(partner, h).wait_recv()
    prepare(near, near_lhs)

    def tiles(ready):
        def late(t):
            ready_tile(t)
            compute(near, near_lhs, t, ready)

        repeat(0, T // 2, lambda t: compute(near, near_lhs, t, ready))
        repeat(T // 2, T - 2, late)
        forward_side()
        repeat(T - 2, T, late)
        arrived(side)
        prepare(side, side_lhs)

    @pl.when(edge)
    def _():
        tiles(((0, 0), (1, 0)))
        repeat(0, T - 2, lambda t: compute(side, side_lhs, t, ((0, 1), (0, 2))))
        forward_diag()
        repeat(T - 2, T, lambda t: compute(side, side_lhs, t, ((0, 1), (0, 2))))
        arrived(diag)
        prepare(diag, far_lhs)
        repeat(0, T, lambda t: compute(diag, far_lhs, t, ((0, 3), (1, 1))))

        def rest(u):
            for c in (2, 3):
                edge_unit(1, c, u).start()

        repeat(0, U, rest)
        send_last(g).start()
        for j in range(1, N):
            s_from = peer(j // 2, j % 2)
            whole_ebuf(s_from).wait_recv()
            send_last(s_from).start()
        repeat(0, n_units // 2, take_back)

    @pl.when(inner)
    def _():
        lag = jnp.where(lower, LAGS[0], LAGS[1])

        def middle(i):
            @pl.when(jnp.logical_and(i >= 0, i < n_units))
            def _():
                take_mid(i)

        def with_side(t):
            compute(side, side_lhs, t)
            take_edge(t)
            middle(t - lag)

        def with_diag(t):
            compute(diag, far_lhs, t)
            take_edge(T + t)
            middle(T + t - lag)

        def both(i):
            take_edge(i)
            middle(i - lag)

        tiles(())
        repeat(0, T - 2, with_side)
        forward_diag()
        repeat(T - 2, T, with_side)
        arrived(diag)
        prepare(diag, far_lhs)
        repeat(0, T, with_diag)
        repeat(2 * T, n_units, both)
        repeat(n_units, n_units + max(LAGS), lambda i: middle(i - lag))

    def put(s):
        band = pl.ds(pl.multiple_of(s * T * W, T * W), T * W)
        return pltpu.make_async_copy(res.at[:, band], res_out.at[:, band], out_sem)

    def finish(s):
        def place(t):
            return pl.ds(pl.multiple_of((s * T + t) * W, W), W)

        @pl.when(edge)
        def _():
            for t in range(T):
                res[:, place(t)] = base[s, t]

        @pl.when(inner)
        def _():
            send_last(s).wait_recv()
            for t in range(T):
                res[:, place(t)] = base[s, t] + last[s, t]

        put(s).start()

    finish(g)

    def collect(j, carry):
        c, i = j // 2, lax.rem(j, 2)
        s = lax.rem(chip // 2 + c // 2, 2) * 2 + lax.rem(lax.rem(chip, 2) + lax.rem(c, 2), 2)
        s = s * 2 + lax.rem(core + i, 2)
        whole_base(s).wait_recv()
        finish(s)
        return carry

    lax.fori_loop(1, N, collect, 0)

    pltpu.make_async_remote_copy(
        src_ref=gathered.at[0:N - 1], dst_ref=gathered.at[0:N - 1], send_sem=ag_send, recv_sem=ag_recv.at[0, 0],
        device_id={"gx": partner}, device_id_type=MESH).wait_send()

    pltpu.make_async_remote_copy(
        src_ref=own.at[0:2], dst_ref=from_edge, send_sem=stream_send, recv_sem=edge_recv.at[0, 0, 0],
        device_id={"row": inward}, device_id_type=MESH).wait_send()

    def sent(ref, sem):
        pltpu.make_async_remote_copy(
            src_ref=ref.at[1:N], dst_ref=ebuf.at[1:N], send_sem=sem, recv_sem=last_recv.at[0],
            device_id={"gx": partner}, device_id_type=MESH).wait_send()

    sent(fin, fin_send)

    @pl.when(edge)
    def _():
        sent(efin, efin_send)
        pltpu.make_async_remote_copy(
            src_ref=ebuf, dst_ref=last, send_sem=last_send, recv_sem=last_recv.at[g],
            device_id={"row": inward}, device_id_type=MESH).wait_send()

    @pl.when(inner)
    def _():
        pltpu.make_async_remote_copy(
            src_ref=own.at[Z - 1], dst_ref=from_in, send_sem=back_send, recv_sem=mid_recv.at[0, 0, 0],
            device_id={"row": outward}, device_id_type=MESH).wait_send()

    pltpu.make_async_copy(res, res_out, out_sem).wait()


def divide(res, pair_occ, occ, energy, res_out, upd_out):
    pk, A = res.shape
    which = lax.broadcasted_iota(jnp.int32, (pk, 1), 0)
    pe = jnp.zeros((pk, 1), jnp.float32)
    for k in range(pk):
        pe = jnp.where(which == k, occ[pair_occ[0, k]] + occ[pair_occ[1, k]], pe)
    v = res[...]
    res_out[...] = v
    upd_out[...] = v / (energy[...] - pe)


def fused_body(N, Z, W, amplitudes, integrals, cd_irrep, ab_irrep, allowed, pair_occ, occ_energy, ab_energy):
    rows, K = amplitudes.shape
    AB = integrals.shape[1]
    A = ab_energy.shape[0]
    T = AB // W
    U = T // 2
    C = N // 2
    pk = rows // Z
    R = 2 * pk
    vmem, smem = pltpu.VMEM, pltpu.SMEM
    f32, bf16, i32 = jnp.float32, jnp.bfloat16, jnp.int32
    dma = pltpu.SemaphoreType.DMA
    out = jax.ShapeDtypeStruct((pk, A), f32)
    residual = pl.pallas_call(
        functools.partial(kernel, N, Z, T, W),
        out_shape=out,
        in_specs=[pl.BlockSpec(memory_space=pltpu.HBM)] * 5,
        out_specs=pl.BlockSpec(memory_space=pltpu.HBM),
        scratch_shapes=[
            smem(cd_irrep.shape, i32), smem(ab_irrep.shape, i32), smem(allowed.shape, i32), dma((3,)), dma,
            vmem((T, K, W), f32), vmem((T, K, W), bf16), vmem((T, K, W), bf16),
            vmem((N, 2, rows // 2, K), f32), vmem((4 * rows, K), f32),
            vmem((4 * rows, K), bf16), vmem((8 * rows, K), bf16), vmem((4 * rows, K), bf16),
            vmem((Z, C, T, R, W), f32), vmem((2, C, T, R, W), f32), vmem((2, C, T, R, W), f32), vmem((C, T, R, W), f32),
            vmem((N, T, pk, W), f32), vmem((N, T, pk, W), f32),
            vmem((N, T, pk, W), f32), vmem((N, T, pk, W), f32), vmem((N, T, pk, W), f32), vmem((pk, A), f32),
            dma((T,)), dma, dma((2, N)), dma, dma((2, C, U)), dma((2, C, U)), dma,
            dma, dma((N,)), dma, dma, dma((N,)), dma,
        ],
        compiler_params=pltpu.CompilerParams(
            collective_id=0, has_side_effects=True, vmem_limit_bytes=VMEM_GRANT),
    )(amplitudes, integrals, cd_irrep, ab_irrep, allowed)
    return pl.pallas_call(
        divide,
        out_shape=(out, out),
        in_specs=[pl.BlockSpec(memory_space=s) for s in (vmem, smem, smem, vmem)],
        out_specs=[pl.BlockSpec(memory_space=vmem)] * 2,
        compiler_params=pltpu.CompilerParams(vmem_limit_bytes=VMEM_GRANT),
    )(residual, pair_occ.T, occ_energy, ab_energy.reshape(1, A))


def solution(mesh):
    N, Z = mesh.shape["gx"], mesh.shape["row"]

    def body(amplitudes, integrals, *rest):
        rows, K = amplitudes.shape
        AB = integrals.shape[1]
        W = 2 * BLK
        pk = rows // Z
        need = 8 * K * AB + 16 * rows * N * K + 16 * rows * N * AB + 28 * pk * AB * N
        if need > VMEM_BUDGET * 3 // 4 or AB % (2 * W) or N != 8 or Z != 4 or rows != 4 * Z:
            return plain_body(amplitudes, integrals, *rest)
        return fused_body(N, Z, W, amplitudes, integrals, *rest)

    return jax.shard_map(
        body,
        mesh=mesh,
        in_specs=(
            P("gx", "row"),
            P("row", "gx"),
            P("row"),
            P("gx"),
            P(),
            P(("gx", "row"), None),
            P(),
            P(),
        ),
        out_specs=(P(("gx", "row"), None), P(("gx", "row"), None)),
        check_vma=False,
    )
```

time: 34.4 us -> 31.9 us (0.927)
  the two profiles are of different devices: /device:TPU:17 before, /device:TPU:0 now
where the time goes in v1:
time: 31.9 us; the launch traced here: 31.8 us
  Pallas kernels  31.1 us (97%)
  between operations  0.64 us (2%)
    pallas_call x1, Pallas kernels, fused_body(): pl.pallas_call(functools.partial(kernel, N, Z, T, W), out_shape=out, in_s...  29.3 us
    pallas_call x1, Pallas kernels, fused_body(): pl.pallas_call(divide, out_shape=(out, out), in_specs=[pl.BlockSpec(memor...  1.78 us

profile of v1, /device:TPU:0, one launch (start us, length us, event | category | flops | bytes accessed | tf_op | source)
XLA Modules:
  0.0 31.8 jit_solution(10340814668762993193)
XLA Ops:
  0.6 29.3 %shard_map.95.res = f32[4,16384]{1,0:T(4,128)} custom-call(f32[16,1024]{1,0:T(8,128)} %amp.1, f32[1024,2048]{1,0:T(8,128)} %integ.1, s32[8]{0:T(128)} %cd_in.1, s32[16]{0:T(128)} %ab_in.1, s32[8,8]{1,0:T(8,128)} %allowed_in.1), custom_call_target="tpu_custom_call" | custom-call | tf_op jit(solution)/shard_map/pallas_call | solution.py:474
  30.0 1.8 %shard_map.96 = (f32[4,16384]{1,0:T(4,128)}, f32[4,16384]{1,0:T(4,128)}) custom-call(f32[4,16384]{1,0:T(4,128)} %shard_map.95.res, s32[2,4]{1,0:T(2,128)} %bitcast.3, f32[100]{0:T(128)} %occ.1, f32[1,16384]{1,0:T(1,128)} %bitcast.2), custom_call_target="tpu_custom_call" | custom-call | tf_op jit(solution)/shard_map/pallas_call | solution.py:493

commit v2 on v1

--- a/solution.py
+++ b/solution.py
@@ -89,7 +89,9 @@
     ]
     for c in small:
         c.start()
-    load(0).start()
+    first, split_first = 1, 2
+    for t in range(first):
+        load(t).start()
     barrier = pltpu.get_barrier_semaphore()
     close = [partner, peer(1, 0), peer(2, 0)]
     for to in close:
@@ -120,20 +122,22 @@
     def spread():
         for h in range(2):
             send_own(partner, h).start()
-        for h in range(2):
-            send_own(across, h).start()
-            send_own(along, h).start()
+        for to, h in ((across, 0), (along, 1), (across, 1), (along, 0)):
+            send_own(to, h).start()
+
+    def forward_cross():
+        relay(across, 0).wait_recv()
+        cross(across, 0, along).start()
+        relay(across, 0).start()
+        relay(along, 1).wait_recv()
+        cross(along, 1, across).start()
+        relay(along, 1).start()
 
     def forward_side():
-        for h in range(2):
-            relay(across, h).wait_recv()
-            if h == 0:
-                cross(across, h, along).start()
-            relay(across, h).start()
-            relay(along, h).wait_recv()
-            if h == 1:
-                cross(along, h, across).start()
-            relay(along, h).start()
+        relay(across, 1).wait_recv()
+        relay(across, 1).start()
+        relay(along, 0).wait_recv()
+        relay(along, 0).start()
 
     def forward_diag():
         for h in range(2):
@@ -308,10 +312,10 @@
     pltpu.make_async_copy(gathered.at[g], gathered.at[g], amp_sem).wait()
     for c in small:
         c.wait()
-    repeat(1, T, lambda t: load(t).start())
+    repeat(first, T, lambda t: load(t).start())
     pl.semaphore_wait(barrier, len(close) + jnp.where(edge, 1, 2))
     spread()
-    repeat(0, T // 2, ready_tile)
+    repeat(0, split_first, ready_tile)
     for h in range(2):
         relay(partner, h).wait_recv()
     prepare(near, near_lhs)
@@ -321,8 +325,10 @@
             ready_tile(t)
             compute(near, near_lhs, t, ready)
 
-        repeat(0, T // 2, lambda t: compute(near, near_lhs, t, ready))
-        repeat(T // 2, T - 2, late)
+        repeat(0, split_first, lambda t: compute(near, near_lhs, t, ready))
+        repeat(split_first, T // 2 + 1, late)
+        forward_cross()
+        repeat(T // 2 + 1, T - 2, late)
         forward_side()
         repeat(T - 2, T, late)
         arrived(side)
@@ -331,9 +337,9 @@
     @pl.when(edge)
     def _():
         tiles(((0, 0), (1, 0)))
-        repeat(0, T - 2, lambda t: compute(side, side_lhs, t, ((0, 1), (0, 2))))
+        repeat(0, T - 3, lambda t: compute(side, side_lhs, t, ((0, 1), (0, 2))))
         forward_diag()
-        repeat(T - 2, T, lambda t: compute(side, side_lhs, t, ((0, 1), (0, 2))))
+        repeat(T - 3, T, lambda t: compute(side, side_lhs, t, ((0, 1), (0, 2))))
         arrived(diag)
         prepare(diag, far_lhs)
         repeat(0, T, lambda t: compute(diag, far_lhs, t, ((0, 3), (1, 1))))
@@ -374,9 +380,9 @@
             middle(i - lag)
 
         tiles(())
-        repeat(0, T - 2, with_side)
+        repeat(0, T - 3, with_side)
         forward_diag()
-        repeat(T - 2, T, with_side)
+        repeat(T - 3, T, with_side)
         arrived(diag)
         prepare(diag, far_lhs)
         repeat(0, T, with_diag)
@@ -508,7 +514,7 @@
         W = 2 * BLK
         pk = rows // Z
         need = 8 * K * AB + 16 * rows * N * K + 16 * rows * N * AB + 28 * pk * AB * N
-        if need > VMEM_BUDGET * 3 // 4 or AB % (2 * W) or N != 8 or Z != 4 or rows != 4 * Z:
+        if need > VMEM_BUDGET * 3 // 4 or AB % (2 * W) or AB < 6 * W or N != 8 or Z != 4 or rows != 4 * Z:
             return plain_body(amplitudes, integrals, *rest)
         return fused_body(N, Z, W, amplitudes, integrals, *rest)
 

time: 31.9 us -> 31.3 us (0.981)
  Pallas kernels: 31.1 us -> 30.5 us
    pallas_call x1, Pallas kernels: 29.3 us -> 28.7 us  [fused_body(): pl.pallas_call(functools.partial(kernel, N, Z, T, W), out_shape=out, in_s...]
where the time goes in v2:
time: 31.3 us; the launch traced here: 31.1 us
  Pallas kernels  30.5 us (97%)
  between operations  0.64 us (2%)
    pallas_call x1, Pallas kernels, fused_body(): pl.pallas_call(functools.partial(kernel, N, Z, T, W), out_shape=out, in_s...  28.7 us
    pallas_call x1, Pallas kernels, fused_body(): pl.pallas_call(divide, out_shape=(out, out), in_specs=[pl.BlockSpec(memor...  1.78 us

profile of v2, /device:TPU:0, one launch (start us, length us, event | category | flops | bytes accessed | tf_op | source)
XLA Modules:
  0.0 31.1 jit_solution(344853546124987037)
XLA Ops:
  0.6 28.7 %shard_map.95.res = f32[4,16384]{1,0:T(4,128)} custom-call(f32[16,1024]{1,0:T(8,128)} %amp.1, f32[1024,2048]{1,0:T(8,128)} %integ.1, s32[8]{0:T(128)} %cd_in.1, s32[16]{0:T(128)} %ab_in.1, s32[8,8]{1,0:T(8,128)} %allowed_in.1), custom_call_target="tpu_custom_call" | custom-call | tf_op jit(solution)/shard_map/pallas_call | solution.py:480
  29.4 1.8 %shard_map.96 = (f32[4,16384]{1,0:T(4,128)}, f32[4,16384]{1,0:T(4,128)}) custom-call(f32[4,16384]{1,0:T(4,128)} %shard_map.95.res, s32[2,4]{1,0:T(2,128)} %bitcast.3, f32[100]{0:T(128)} %occ.1, f32[1,16384]{1,0:T(1,128)} %bitcast.2), custom_call_target="tpu_custom_call" | custom-call | tf_op jit(solution)/shard_map/pallas_call | solution.py:499

commit v3 on v2

--- a/solution.py
+++ b/solution.py
@@ -180,10 +180,18 @@
                 wh[t, b * BLK:(b + 1) * BLK, j * BLK:(j + 1) * BLK] = hi
                 wl[t, b * BLK:(b + 1) * BLK, j * BLK:(j + 1) * BLK] = (x - hi.astype(jnp.float32)).astype(jnp.bfloat16)
 
-    def send_piece(c, i, t):
-        return pltpu.make_async_remote_copy(
-            src_ref=efin.at[c * 2 + i, t], dst_ref=ebuf.at[g, t], send_sem=efin_send, recv_sem=last_recv.at[g],
-            device_id={"gx": peer(c, i)}, device_id_type=MESH)
+    def send_piece(c, i, u):
+        return pltpu.make_async_remote_copy(
+            src_ref=efin.at[c * 2 + i, pair(u)], dst_ref=ebuf.at[g, pair(u)], send_sem=efin_send,
+            recv_sem=last_recv.at[g], device_id={"gx": peer(c, i)}, device_id_type=MESH)
+
+    def exchange(u):
+        for c in range(C):
+            both = own[2, c, pair(u)]
+            for i in range(2):
+                if c or i:
+                    efin[c * 2 + i, pair(u)] = both[:, i * pk:(i + 1) * pk, :]
+                    send_piece(c, i, u).start()
 
     def send_tile(k, c, t):
         return pltpu.make_async_remote_copy(
@@ -208,18 +216,14 @@
 
         for k, c in ready:
             send_tile(k, c, t).start()
-        if ready:
-            for j, c in enumerate(cs):
-                for i in range(2):
-                    at = ((2 * n + j) * 2 + i) * pk
-                    if c == 0 and i == 0:
-                        ebuf[g, t] = total[at:at + pk, :]
-                    else:
-                        efin[c * 2 + i, t] = total[at:at + pk, :]
-                        send_piece(c, i, t).start()
+        if ready and cs[0] == 0:
+            at = 4 * n * pk
+            ebuf[g, t] = total[at:at + pk, :]
 
     def unit(i):
-        seg, u, b = i // (2 * U), lax.rem(i, 2 * U) // 2, lax.rem(i, 2)
+        seg, r = i // (2 * U), lax.rem(i, 2 * U)
+        u = jnp.where(seg == 2, lax.rem(r, U), r // 2)
+        b = jnp.where(seg == 2, r // U, lax.rem(r, 2))
         k = jnp.where(seg == 0, b, jnp.where(seg == 1, 0, jnp.where(seg == 2, b, 1)))
         c = jnp.where(seg == 0, 0, jnp.where(seg == 1, 1 + b, jnp.where(seg == 2, 3 - 2 * b, 2 + b)))
         return k, c, u
@@ -342,14 +346,16 @@
         repeat(T - 3, T, lambda t: compute(side, side_lhs, t, ((0, 1), (0, 2))))
         arrived(diag)
         prepare(diag, far_lhs)
-        repeat(0, T, lambda t: compute(diag, far_lhs, t, ((0, 3), (1, 1))))
+        send_last(g).start()
+        repeat(0, T, lambda t: compute(diag, far_lhs, t, ((0, 3),)))
 
         def rest(u):
             for c in (2, 3):
                 edge_unit(1, c, u).start()
 
+        repeat(0, U, lambda u: edge_unit(1, 1, u).start())
         repeat(0, U, rest)
-        send_last(g).start()
+        repeat(0, U, exchange)
         for j in range(1, N):
             s_from = peer(j // 2, j % 2)
             whole_ebuf(s_from).wait_recv()

time: 31.3 us -> 30.7 us (0.981)
  Pallas kernels: 30.5 us -> 29.9 us
    pallas_call x1, Pallas kernels: 28.7 us -> 28.1 us  [fused_body(): pl.pallas_call(functools.partial(kernel, N, Z, T, W), out_shape=out, in_s...]
where the time goes in v3:
time: 30.7 us; the launch traced here: 30.5 us
  Pallas kernels  29.9 us (97%)
  between operations  0.64 us (2%)
    pallas_call x1, Pallas kernels, fused_body(): pl.pallas_call(functools.partial(kernel, N, Z, T, W), out_shape=out, in_s...  28.1 us
    pallas_call x1, Pallas kernels, fused_body(): pl.pallas_call(divide, out_shape=(out, out), in_specs=[pl.BlockSpec(memor...  1.78 us

profile of v3, /device:TPU:0, one launch (start us, length us, event | category | flops | bytes accessed | tf_op | source)
XLA Modules:
  0.0 30.5 jit_solution(849805129243900896)
XLA Ops:
  0.6 28.1 %shard_map.95.res = f32[4,16384]{1,0:T(4,128)} custom-call(f32[16,1024]{1,0:T(8,128)} %amp.1, f32[1024,2048]{1,0:T(8,128)} %integ.1, s32[8]{0:T(128)} %cd_in.1, s32[16]{0:T(128)} %ab_in.1, s32[8,8]{1,0:T(8,128)} %allowed_in.1), custom_call_target="tpu_custom_call" | custom-call | tf_op jit(solution)/shard_map/pallas_call | solution.py:486
  28.7 1.8 %shard_map.96 = (f32[4,16384]{1,0:T(4,128)}, f32[4,16384]{1,0:T(4,128)}) custom-call(f32[4,16384]{1,0:T(4,128)} %shard_map.95.res, s32[2,4]{1,0:T(2,128)} %bitcast.3, f32[100]{0:T(128)} %occ.1, f32[1,16384]{1,0:T(1,128)} %bitcast.2), custom_call_target="tpu_custom_call" | custom-call | tf_op jit(solution)/shard_map/pallas_call | solution.py:505
